TPU v7x, 32 devices: a whole 2x2x4 slice. The times are simulated.
32 devices in a mesh: prompt: 2 (over y), tensor: 4 (over z), ctx: 4 (over x, core).
Axes of the slice: x: 2, y: 2, z: 4, core: 2. Of those that a mesh axis runs over, the one named last changes fastest.
Arguments:
- hidden_in: bfloat16 [2048, 8192], P(('prompt', 'ctx', 'tensor')), parts along dimension 0, may hold values from -6 to 6
- norm_gain: float32 [8192], replicated, may hold values from 0.1 to 1.9
- weight_in: bfloat16 [8192, 3, 4096], P('ctx', None, 'tensor'), may hold values from -0.0625 to 0.0625
- filter_taps: float32 [256, 128], P('tensor'), may hold values from -0.6 to 0.6
- filter_decay: float32 [256], P('tensor'), may hold values from 0.003 to 0.3
- skip_gain: float32 [4096], P('tensor'), may hold values from -1 to 1
- tail_cache: bfloat16 [254, 4096], P('prompt', 'tensor'), parts along dimension 0, may hold values from -6 to 6
- output_weight: bfloat16 [4096, 8192], P(None, 'tensor'), may hold values from -0.09375 to 0.09375
Outputs:
- mixer_output: bfloat16 [2048, 8192], P(('prompt', 'ctx'), 'tensor'), parts along dimension 0
There are 2 independent parts, one for each index of `prompt`. A program takes and returns all parts, laid end to end along the dimension named above; an argument that names none is the same for every part. Nothing has to cross between parts.
All inputs are finite; a program needn't handle non-finite values.
Results may differ from a plain program's by a relative error of at most 0.0095.
Values may be sent and summed in bfloat16 or wider, within the bound.
A program may use at most 256 MiB of HBM per device.

v0:
```python
import jax
import jax.numpy as jnp
from jax import lax
from jax.sharding import PartitionSpec as P

GROUP = 16


def passed_along(value, axis, steps):
    count = lax.axis_size(axis)
    leading, last = (max(0, -steps), min(count, count - steps))
    return lax.ppermute(value, axis, [(source, source + steps) for source in range(leading, last)])


def normalize_rows(hidden_in, norm_gain):
    values = hidden_in.astype(jnp.float32)
    scaled = lax.rsqrt(jnp.mean(values * values, axis=-1, keepdims=True) + 1e-06)
    return (values * scaled * norm_gain[None, :]).astype(jnp.bfloat16)


def banded_taps(taps_full, shard_rows):
    group_count, tap_count = taps_full.shape
    width = shard_rows + tap_count - 1
    first_row = jnp.concatenate(
        [taps_full[:, ::-1], jnp.zeros((group_count, width + 1 - tap_count), jnp.float32)], axis=1
    )
    repeated = jnp.tile(first_row, (1, shard_rows))
    return repeated[:, : shard_rows * width].reshape(group_count, shard_rows, width)


def on_device(
    hidden_in, norm_gain, weight_in, filter_taps, filter_decay, skip_gain, tail_cache, output_weight
):
    gathered = lax.all_gather(hidden_in, "tensor", axis=0, tiled=True)
    normed = normalize_rows(gathered, norm_gain)
    shard_rows = normed.shape[0]
    channels = weight_in.shape[2]
    qkv = jnp.einsum(
        "td,dgc->tgc",
        normed,
        lax.all_gather(weight_in, "ctx", axis=0, tiled=True),
        preferred_element_type=jnp.float32,
    )
    query = qkv[:, 0]
    product = (qkv[:, 1] * qkv[:, 2]).astype(jnp.bfloat16)
    tail_rows = filter_taps.shape[1] - 1
    incoming = passed_along(product[shard_rows - tail_rows :], "ctx", 1)
    leading = lax.axis_index("ctx") == 0
    before = jnp.where(leading, tail_cache, incoming)
    extended = jnp.concatenate([before, product], axis=0).astype(jnp.float32)
    lags = jnp.arange(filter_taps.shape[1]).astype(jnp.float32)
    taps_full = filter_taps * jnp.exp(-filter_decay[:, None] * lags[None, :])
    band = banded_taps(taps_full, shard_rows)
    group_count = taps_full.shape[0]
    grouped = extended.reshape(extended.shape[0], group_count, GROUP)
    filtered = jnp.einsum(
        "gsj,jgi->sgi",
        band,
        grouped,
        precision=lax.Precision.HIGHEST,
        preferred_element_type=jnp.float32,
    ).reshape(shard_rows, channels)
    gated = (query * (filtered + skip_gain[None, :] * product.astype(jnp.float32))).astype(
        jnp.bfloat16
    )
    totals = jnp.dot(
        lax.all_gather(gated, "tensor", axis=1, tiled=True),
        output_weight,
        preferred_element_type=jnp.float32,
    )
    return totals.astype(jnp.bfloat16)


def solution(mesh):
    in_specs = (
        P(("prompt", "ctx", "tensor"), None),
        P(),
        P("ctx", None, "tensor"),
        P("tensor", None),
        P("tensor"),
        P("tensor"),
        P("prompt", "tensor"),
        P(None, "tensor"),
    )
    out_specs = P(("prompt", "ctx"), "tensor")
    return jax.shard_map(
        on_device, mesh=mesh, in_specs=in_specs, out_specs=out_specs, check_vma=False
    )
```

profile of v0, /device:TPU:0, one launch (start us, length us, event | category | flops | bytes accessed | tf_op | source)
XLA Modules:
  0.0 509.6 jit_solution(4066531910178312621)
XLA Ops:
  6.5 0.7 all-gather.4.cloned.1.call-update
  7.3 0.7 all-gather.6.cloned.1.call-update
  8.1 0.1 exponential_multiply_fusion
  8.2 0.1 rev.3
  8.3 10.3 %tile.4 = f32[64,256,384]{2,1,0:T(8,128)} broadcast(f32[64,384]{1,0:T(8,128)S(1)} %concatenate.7), dimensions={0,2} | broadcast | bytes 25264128 | tf_op jit(solution)/shard_map/tile | solution.py:27
  18.6 22.1 %copy.13 = f32[8,8,256,384]{3,1,2,0:T(8,128)S(1)} copy(f32[8,8,256,384]{3,2,1,0:T(8,128)} %bitcast.25) | data formatting | bytes 50331648
  40.7 8.6 %slice.28 = f32[64,98048]{1,0:T(8,128)} slice(f32[64,98304]{1,0:T(8,128)S(1)} %bitcast.26), slice={[0:64], [0:98048]} | slice | bytes 50200576 | tf_op jit(solution)/shard_map/slice | solution.py:28
  49.3 32.8 %reshape.33 = f32[64,256,383]{2,1,0:T(8,128)} reshape(f32[64,98048]{1,0:T(8,128)} %slice.28) | data formatting | bytes 50200576 | tf_op jit(solution)/shard_map/reshape | solution.py:28
  82.1 10.3 %all-gather.4.cloned.1.call-done = bf16[256,8192]{1,0:T(8,128)(2,1)} async-done(((bf16[64,8192]{1,0:T(8,128)(2,1)}), bf16[256,8192]{1,0:T(8,128)(2,1)}) %all-gather.4.cloned.1.call-update) | async-done | bytes 4194320 | tf_op jit(solution)/shard_map/all_gather | solution.py:34
  92.4 3.1 fusion
  95.5 294.1 %all-gather.6.cloned.1.call-done = bf16[8192,3,1024]{2,0,1:T(8,128)(2,1)} async-done(((bf16[2048,3,1024]{2,0,1:T(8,128)(2,1)}), bf16[8192,3,1024]{2,0,1:T(8,128)(2,1)}) %all-gather.6.cloned.1.call-update) | async-done | bytes 50331664 | tf_op jit(solution)/shard_map/all_gather | solution.py:41
  389.7 21.9 %fusion.4 = f32[256,3,1024]{2,0,1:T(8,128)S(1)} fusion(bf16[8192,3,1024]{2,0,1:T(8,128)(2,1)} %all-gather.6.cloned.1.call-done, bf16[256,8192]{1,0:T(8,128)(2,1)} %all-gather.4.cloned.1.call-done, f32[8192]{0:T(1024)S(1)} %copy-done.3, f32[256]{0:T(256)S(1)} %add_rsqrt_fusion), kind=kOutput, calls=%fused_computation.6 | convolution fusion | flops 12893290496 | bytes 57705472 | tf_op jit(solution)/shard_map/td,dgc->tgc/dot_general | solution.py:38
  411.6 0.1 fusion.8
  411.8 0.1 slice_bitcast_fusion.1
  411.8 2.4 collective-permute-start
  414.2 0.1 fusion.17
  414.3 0.8 collective-permute-done
  415.2 1.0 pad_maximum_fusion
  416.2 2.3 copy.11
  418.5 17.3 %fusion.11 = f32[64,16,256]{2,1,0:T(8,128)} fusion(bf16[383,64,16]{0,2,1:T(8,128)(2,1)} %bitcast.28, f32[64,256,383]{2,1,0:T(8,128)} %reshape.33), kind=kOutput, calls=%fused_computation.21 | convolution fusion | flops 1204813824 | bytes 26933248 | tf_op jit(solution)/shard_map/gsj,jgi->sgi/dot_general | solution.py:56
  435.8 2.5 copy.12
  438.3 2.4 fusion.10
  440.8 50.5 %all-gather.8.cloned.1.call-done = bf16[256,4096]{1,0:T(8,128)(2,1)} async-done(((bf16[256,1024]{1,0:T(8,128)(2,1)}), bf16[256,4096]{1,0:T(8,128)(2,1)}) %all-gather.8.cloned.1.call-update) | async-done | bytes 2097168 | tf_op jit(solution)/shard_map/all_gather | solution.py:67
  491.2 11.9 %convolution_convert_fusion = bf16[256,2048]{1,0:T(8,128)(2,1)} fusion(bf16[256,4096]{1,0:T(8,128)(2,1)} %all-gather.8.cloned.1.call-done, bf16[4096,2048]{1,0:T(8,128)(2,1)} %param.15), kind=kOutput, calls=%fused_computation.9 | convolution fusion | flops 4295491584 | bytes 19922944 | tf_op jit(solution)/shard_map/dot_general | solution.py:66
  (19 shorter events, 0.2 us)
Async XLA Ops:
  6.5 1.5 copy-start.4
  6.5 1.6 copy-start.1
  6.5 85.9 %all-gather.4.cloned.1.call-start = ((), (), s32[]{:S(2)}) async-start(), calls=%async_computation | async-start | bytes 5242880 | tf_op jit(solution)/shard_map/all_gather | solution.py:34
  7.3 382.4 %all-gather.6.cloned.1.call-start = ((), (), s32[]{:S(2)}) async-start(), calls=%async_computation.1 | async-start | bytes 62914560 | tf_op jit(solution)/shard_map/all_gather | solution.py:41
  8.0 483.2 %all-gather.8.cloned.1.call-start = ((), (), s32[]{:S(2)}) async-start(), calls=%async_computation.2 | async-start | bytes 2621440 | tf_op jit(solution)/shard_map/all_gather | solution.py:67
  49.3 340.4 %copy-start.3 = (f32[8192]{0:T(1024)S(1)}, f32[8192]{0:T(1024)}, u32[]{:S(2)}) copy-start(f32[8192]{0:T(1024)} %param.9) | copy-start | bytes 98308
  95.5 319.6 %copy-start = (bf16[127,1024]{1,0:T(8,128)(2,1)S(1)}, bf16[127,1024]{1,0:T(8,128)(2,1)}, u32[]{:S(2)}) copy-start(bf16[127,1024]{1,0:T(8,128)(2,1)} %param.14) | copy-start | bytes 780292
  411.8 3.3 collective-permute-start
  418.5 19.8 %copy-start.2 = (f32[1024]{0:T(1024)S(1)}, f32[1024]{0:T(1024)}, u32[]{:S(2)}) copy-start(f32[1024]{0:T(1024)} %param.13) | copy-start | bytes 12292
Sparse Core Ops, SparseCore 0:
  8.9 83.4 all-gather.3
  94.0 295.6 all-gather.5
  440.9 50.3 all-gather.7
where the time goes:
time: 510 us
  waiting for transfers between devices  357 us (70%)
  local copies, waits for them, and re-layouts  78.8 us (15%)
  matrix products  51.1 us (10%)
  between operations  13.2 us (3%)
  other arithmetic  6.97 us (1%)
    all_gather x1, waiting for transfers between devices, on_device(): lax.all_gather(weight_in, 'ctx', axis=0, tiled=True)  294 us
    all_gather x1, waiting for transfers between devices, on_device(): lax.all_gather(gated, 'tensor', axis=1, tiled=True)  50.5 us
    reshape x1, local copies, waits for them, and re-layouts, banded_taps(): repeated[:, :shard_rows * width].reshape(group_count, shard_rows, width)  32.8 us
    unnamed x11, local copies, waits for them, and re-layouts  22.1 us
    dot_general x1, matrix products, on_device(): jnp.einsum('td,dgc->tgc', normed, lax.all_gather(weight_in, 'ctx', axis=0...  21.9 us
    dot_general x1, matrix products, on_device(): jnp.einsum('gsj,jgi->sgi', band, grouped, precision=lax.Precision.HIGHEST...  17.3 us
    dot_general x1, matrix products, on_device(): jnp.dot(lax.all_gather(gated, 'tensor', axis=1, tiled=True), output_weigh...  11.9 us
    another operation x1, local copies, waits for them, and re-layouts, banded_taps(): repeated = jnp.tile(first_row, (1, shard_rows))  10.3 us
  transfers between devices with their start and end apart: 4, of which 4 were waited for; matrix products, arithmetic and copies ran while one was open for 15% of the time, Pallas kernels for 0%

commit v1 on v0

--- a/solution.py
+++ b/solution.py
@@ -35,12 +35,20 @@
     normed = normalize_rows(gathered, norm_gain)
     shard_rows = normed.shape[0]
     channels = weight_in.shape[2]
-    qkv = jnp.einsum(
-        "td,dgc->tgc",
-        normed,
-        lax.all_gather(weight_in, "ctx", axis=0, tiled=True),
-        preferred_element_type=jnp.float32,
-    )
+    size, mine, rows = (lax.axis_size("ctx"), lax.axis_index("ctx"), weight_in.shape[0])
+    forward = [(i, (i + 1) % size) for i in range(size)]
+    held, so_far = (weight_in, None)
+    for lap in range(size):
+        upcoming = lax.ppermute(held, "ctx", forward) if lap < size - 1 else None
+        absorb = jnp.einsum(
+            "td,dgc->tgc",
+            lax.dynamic_slice_in_dim(normed, (mine - lap) % size * rows, held.shape[0], axis=1),
+            held,
+            preferred_element_type=jnp.float32,
+        )
+        so_far = absorb if so_far is None else so_far + absorb
+        held = upcoming
+    qkv = so_far
     query = qkv[:, 0]
     product = (qkv[:, 1] * qkv[:, 2]).astype(jnp.bfloat16)
     tail_rows = filter_taps.shape[1] - 1

time: 510 us -> 533 us (1.045)
  waiting for transfers between devices: 357 us -> 370 us
  local copies, waits for them, and re-layouts: 78.8 us -> 84.5 us
    ppermute x0 -> x3, waiting for transfers between devices: none -> 309 us  [on_device(): upcoming = lax.ppermute(held, 'ctx', forward) if lap < size - 1 else None]
    all_gather x1 -> x0, waiting for transfers between devices: 294 us -> none  [on_device(): lax.all_gather(weight_in, 'ctx', axis=0, tiled=True)]
    unnamed x11 -> x17, local copies, waits for them, and re-layouts: 22.1 us -> 27 us
    dot_general x1 -> x4, matrix products: 21.9 us -> 23.3 us  [on_device(): jnp.einsum('td,dgc->tgc', lax.dynamic_slice_in_dim(normed, (mine - lap) %...]
  transfers between devices with their start and end apart: 4 -> 6, of which waited for: 4 -> 6; matrix products, arithmetic and copies ran while one was open for 15% -> 18% of each run, Pallas kernels for 0% -> 0%
where the time goes in v1:
time: 533 us
  waiting for transfers between devices  370 us (69%)
  local copies, waits for them, and re-layouts  84.5 us (16%)
  matrix products  52.5 us (10%)
  between operations  13.6 us (3%)
  other arithmetic  9.71 us (2%)
    ppermute x3, waiting for transfers between devices, on_device(): upcoming = lax.ppermute(held, 'ctx', forward) if lap < size - 1 else None  309 us
    all_gather x1, waiting for transfers between devices, on_device(): lax.all_gather(gated, 'tensor', axis=1, tiled=True)  52.9 us
    reshape x1, local copies, waits for them, and re-layouts, banded_taps(): repeated[:, :shard_rows * width].reshape(group_count, shard_rows, width)  32.8 us
    unnamed x17, local copies, waits for them, and re-layouts  27 us
    dot_general x4, matrix products, on_device(): jnp.einsum('td,dgc->tgc', lax.dynamic_slice_in_dim(normed, (mine - lap) %...  23.3 us
    dot_general x1, matrix products, on_device(): jnp.einsum('gsj,jgi->sgi', band, grouped, precision=lax.Precision.HIGHEST...  17.3 us
    dot_general x1, matrix products, on_device(): jnp.dot(lax.all_gather(gated, 'tensor', axis=1, tiled=True), output_weigh...  11.9 us
    another operation x1, local copies, waits for them, and re-layouts, banded_taps(): repeated = jnp.tile(first_row, (1, shard_rows))  11 us
  transfers between devices with their start and end apart: 6, of which 6 were waited for; matrix products, arithmetic and copies ran while one was open for 18% of the time, Pallas kernels for 0%

profile of v1, /device:TPU:0, one launch (start us, length us, event | category | flops | bytes accessed | tf_op | source)
XLA Modules:
  0.0 532.9 jit_solution(17255041775555120461)
XLA Ops:
  7.0 138.2 %collective-permute-done = bf16[2048,3,1024]{2,0,1:T(8,128)(2,1)S(1)} collective-permute-done((bf16[2048,3,1024]{2,0,1:T(8,128)(2,1)}, bf16[2048,3,1024]{2,0,1:T(8,128)(2,1)S(1)}, u32[]{:S(2)}, u32[]{:S(2)}) %collective-permute-start) | collective-permute-done | bytes 12582944 | tf_op jit(solution)/shard_map/ppermute | solution.py:42
  145.2 4.5 copy-done
  149.7 137.9 %collective-permute-done.1 = bf16[2048,3,1024]{2,0,1:T(8,128)(2,1)} collective-permute-done((bf16[2048,3,1024]{2,0,1:T(8,128)(2,1)S(1)}, bf16[2048,3,1024]{2,0,1:T(8,128)(2,1)}, u32[]{:S(2)}, u32[]{:S(2)}) %collective-permute-start.1) | collective-permute-done | bytes 12582944 | tf_op jit(solution)/shard_map/ppermute | solution.py:42
  289.3 11.0 %tile.4 = f32[64,256,384]{2,1,0:T(8,128)} broadcast(f32[64,384]{1,0:T(8,128)S(1)} %concatenate.7), dimensions={0,2} | broadcast | bytes 25264128 | tf_op jit(solution)/shard_map/tile | solution.py:27
  300.3 21.8 %copy.13 = f32[8,8,256,384]{3,1,2,0:T(8,128)S(1)} copy(f32[8,8,256,384]{3,2,1,0:T(8,128)} %bitcast.37) | data formatting | bytes 50331648
  322.1 8.6 %slice.28 = f32[64,98048]{1,0:T(8,128)} slice(f32[64,98304]{1,0:T(8,128)S(1)} %bitcast.38), slice={[0:64], [0:98048]} | slice | bytes 50200576 | tf_op jit(solution)/shard_map/slice | solution.py:28
  330.7 32.8 %reshape.33 = f32[64,256,383]{2,1,0:T(8,128)} reshape(f32[64,98048]{1,0:T(8,128)} %slice.28) | data formatting | bytes 50200576 | tf_op jit(solution)/shard_map/reshape | solution.py:28
  363.6 7.3 %all-gather.3.cloned.1.call-done = bf16[256,8192]{1,0:T(8,128)(2,1)} async-done(((bf16[64,8192]{1,0:T(8,128)(2,1)}), bf16[256,8192]{1,0:T(8,128)(2,1)}) %all-gather.3.cloned.1.call-update) | async-done | bytes 4194320 | tf_op jit(solution)/shard_map/all_gather | solution.py:34
  370.9 3.3 fusion
  374.4 1.2 fusion.2
  375.6 6.8 %fusion.11 = f32[256,3,1024]{2,0,1:T(8,128)S(1)} fusion(bf16[2048,3,1024]{2,0,1:T(8,128)(2,1)} %param.10, bf16[256,8192]{1,0:T(8,128)(2,1)S(1)} %fusion.2, s32[]{:T(128)S(6)} %select_n.40), kind=kOutput, calls=%fused_computation.17 | convolution fusion | flops 3221225472 | bytes 16777220 | tf_op jit(solution)/shard_map/td,dgc->tgc/dot_general | solution.py:43
  382.9 3.5 fusion.9
  386.4 6.4 %fusion.7 = f32[256,3,1024]{2,0,1:T(8,128)S(1)} fusion(bf16[2048,3,1024]{2,0,1:T(8,128)(2,1)} %collective-permute-done.1, bf16[256,8192]{1,0:T(8,128)(2,1)S(1)} %fusion.2, s32[]{:T(128)S(6)} %select_n.44), kind=kOutput, calls=%fused_computation.13 | convolution fusion | flops 3221225472 | bytes 16777220 | tf_op jit(solution)/shard_map/td,dgc->tgc/dot_general | solution.py:43
  392.8 32.9 %collective-permute-done.2 = bf16[2048,3,1024]{2,0,1:T(8,128)(2,1)} collective-permute-done((bf16[2048,3,1024]{2,0,1:T(8,128)(2,1)}, bf16[2048,3,1024]{2,0,1:T(8,128)(2,1)}, u32[]{:S(2)}, u32[]{:S(2)}) %collective-permute-start.2) | collective-permute-done | bytes 12582944 | tf_op jit(solution)/shard_map/ppermute | solution.py:42
  425.7 6.6 %add_add_fusion = f32[256,3,1024]{2,0,1:T(8,128)S(1)} fusion(f32[256,3,1024]{2,0,1:T(8,128)S(1)} %fusion.7, f32[256,3,1024]{2,0,1:T(8,128)S(1)} %fusion.11, f32[256,3,1024]{2,0,1:T(8,128)S(1)} %fusion.9, bf16[2048,3,1024]{2,0,1:T(8,128)(2,1)} %collective-permute-done.2, bf16[256,8192]{1,0:T(8,128)(2,1)S(1)} %fusion.2, s32[]{:T(128)S(6)} %select_n.46), kind=kOutput, calls=%fused_computation.5 | convolution fusion | flops 3223584768 | bytes 26214404 | tf_op jit(solution)/shard_map/td,dgc->tgc/dot_general | solution.py:43
  432.6 1.9 collective-permute-start.3
  434.6 1.0 collective-permute-done.3
  435.6 1.0 pad_maximum_fusion
  436.6 2.4 copy.11
  439.0 17.3 %fusion.21 = f32[64,16,256]{2,1,0:T(8,128)} fusion(bf16[383,64,16]{0,2,1:T(8,128)(2,1)} %bitcast.42, f32[64,256,383]{2,1,0:T(8,128)} %reshape.33), kind=kOutput, calls=%fused_computation.33 | convolution fusion | flops 1204813824 | bytes 26933248 | tf_op jit(solution)/shard_map/gsj,jgi->sgi/dot_general | solution.py:64
  456.3 2.5 copy.12
  458.8 2.4 fusion.5
  461.3 52.9 %all-gather.5.cloned.1.call-done = bf16[256,4096]{1,0:T(8,128)(2,1)} async-done(((bf16[256,1024]{1,0:T(8,128)(2,1)}), bf16[256,4096]{1,0:T(8,128)(2,1)}) %all-gather.5.cloned.1.call-update) | async-done | bytes 2097168 | tf_op jit(solution)/shard_map/all_gather | solution.py:75
  514.2 11.9 %convolution_convert_fusion = bf16[256,2048]{1,0:T(8,128)(2,1)} fusion(bf16[256,4096]{1,0:T(8,128)(2,1)} %all-gather.5.cloned.1.call-done, bf16[4096,2048]{1,0:T(8,128)(2,1)} %param.15), kind=kOutput, calls=%fused_computation.6 | convolution fusion | flops 4295491584 | bytes 19922944 | tf_op jit(solution)/shard_map/dot_general | solution.py:74
  (33 shorter events, 3.2 us)
Async XLA Ops:
  6.5 364.4 %all-gather.3.cloned.1.call-start = ((), (), s32[]{:S(2)}) async-start(), calls=%async_computation | async-start | bytes 5242880 | tf_op jit(solution)/shard_map/all_gather | solution.py:34
  6.5 138.7 %collective-permute-start = (bf16[2048,3,1024]{2,0,1:T(8,128)(2,1)}, bf16[2048,3,1024]{2,0,1:T(8,128)(2,1)S(1)}, u32[]{:S(2)}, u32[]{:S(2)}) collective-permute-start(bf16[2048,3,1024]{2,0,1:T(8,128)(2,1)} %param.10), channel_id=1, source_target_pairs={{0,1},{1,2},{2,3},{3,0},{4,5},{5,6},{6,7},{7,4},{8,9},{9,10},{10,1... | collective-permute-start | bytes 37748744 | tf_op jit(solution)/shard_map/ppermute | solution.py:42
  145.2 4.5 copy-start
  149.7 137.9 %collective-permute-start.1 = (bf16[2048,3,1024]{2,0,1:T(8,128)(2,1)S(1)}, bf16[2048,3,1024]{2,0,1:T(8,128)(2,1)}, u32[]{:S(2)}, u32[]{:S(2)}) collective-permute-start(bf16[2048,3,1024]{2,0,1:T(8,128)(2,1)S(1)} %collective-permute-done), channel_id=1, source_target_pairs={{0,1},{1,2},{2,3},{3,0},{4,5},{5,6},{6,7},{7,4},{8,9},{9,10},{10,1... | collective-permute-start | bytes 37748744 | tf_op jit(solution)/shard_map/ppermute | solution.py:42
  287.6 138.1 %collective-permute-start.2 = (bf16[2048,3,1024]{2,0,1:T(8,128)(2,1)}, bf16[2048,3,1024]{2,0,1:T(8,128)(2,1)}, u32[]{:S(2)}, u32[]{:S(2)}) collective-permute-start(bf16[2048,3,1024]{2,0,1:T(8,128)(2,1)} %collective-permute-done.1), channel_id=1, source_target_pairs={{0,1},{1,2},{2,3},{3,0},{4,5},{5,6},{6,7},{7,4},{8,9},{9,10},{10,1... | collective-permute-start | bytes 37748744 | tf_op jit(solution)/shard_map/ppermute | solution.py:42
  287.6 226.5 %all-gather.5.cloned.1.call-start = ((), (), s32[]{:S(2)}) async-start(), calls=%async_computation.1 | async-start | bytes 2621440 | tf_op jit(solution)/shard_map/all_gather | solution.py:75
  330.7 43.5 %copy-start.3 = (f32[8192]{0:T(1024)S(1)}, f32[8192]{0:T(1024)}, u32[]{:S(2)}) copy-start(f32[8192]{0:T(1024)} %param.9) | copy-start | bytes 98308
  370.9 3.4 copy-start.1
  374.4 8.0 %slice-start = ((s8[12582912]{0:T(1024)(128)(4,1)}), s8[4194304]{0:T(1024)(128)(4,1)S(1)}, s32[]{:S(2)}) async-start(s8[12582912]{0:T(1024)(128)(4,1)} %bitcast.39), calls=%async_computation.2 | async-start | bytes 8388608
  375.6 6.8 %slice-start.1 = ((s8[12582912]{0:T(1024)(128)(4,1)}), s8[4194304]{0:T(1024)(128)(4,1)S(1)}, s32[]{:S(2)}) async-start(s8[12582912]{0:T(1024)(128)(4,1)} %bitcast.39), calls=%async_computation.3 | async-start | bytes 8388608
  375.6 7.3 %slice-start.2 = ((s8[12582912]{0:T(1024)(128)(4,1)}), s8[4194304]{0:T(1024)(128)(4,1)S(1)}, s32[]{:S(2)}) async-start(s8[12582912]{0:T(1024)(128)(4,1)} %bitcast.39), calls=%async_computation.4 | async-start | bytes 8388608
  432.4 3.2 copy-start.2
  432.6 3.0 collective-permute-start.3
  439.0 19.8 %copy-start.4 = (f32[1024]{0:T(1024)S(1)}, f32[1024]{0:T(1024)}, u32[]{:S(2)}) copy-start(f32[1024]{0:T(1024)} %param.13) | copy-start | bytes 12292
Sparse Core Ops, SparseCore 0:
  287.7 83.1 all-gather.2
  461.4 52.6 all-gather.4
